TPU v7x, 32 devices: a whole 2x2x4 slice. The times are simulated.
32 devices in a mesh: groups: 2 (over y), section: 2 (over core), row: 2 (over x), col: 4 (over z).
Axes of the slice: x: 2, y: 2, z: 4, core: 2. Of those that a mesh axis runs over, the one named last changes fastest.
Arguments:
- hidden: bfloat16 [2, 2, 3072, 8192], P('section', None, ('groups', 'col'), 'row'), parts along dimension 2, may hold values from -400 to 400
- upstream: bfloat16 [2, 3072, 8192], P(None, ('groups', 'col'), 'row'), parts along dimension 1, may hold values from -8 to 8
- weights: bfloat16 [2, 8192, 8192], P('section', 'row', 'col'), may hold values from -0.0625 to 0.0625
- norm_gains: bfloat16 [2, 8192], P('section', 'row'), may hold values from 0.5 to 1.5
- steering: bfloat16 [16384], P(('groups', 'row')), parts along dimension 0, may hold values from -18 to 18
- steer_layer: int32 [2, 3072], P(None, ('groups', 'col')), parts along dimension 1, may hold values from 0 to 1
Outputs:
- section_grads: bfloat16 [2, 2, 3072, 8192], P('section', None, ('groups', 'col'), 'row'), parts along dimension 2
- steer_grad: float32 [16384], P(('groups', 'row')), parts along dimension 0
There are 2 independent parts, one for each index of `groups`. A program takes and returns all parts, laid end to end along the dimension named above; an argument that names none is the same for every part. Nothing has to cross between parts.
All inputs are finite; a program needn't handle non-finite values.
Results may differ from a plain program's by a relative error of at most 0.0038.
Values may be sent and summed in bfloat16 or wider, within the bound.
A program may use at most 320 MiB of HBM per device.

v0:
```python
import jax
import jax.numpy as jnp
from jax import lax
from jax.sharding import PartitionSpec as P

D = 8192
ROWS = 1536
MICRO = 2
epsilon = 1e-06


def passed_along(value, axis, steps):
    count = lax.axis_size(axis)
    initial, last = (max(0, -steps), min(count, count - steps))
    return lax.ppermute(value, axis, [(source, source + steps) for source in range(initial, last)])


def local(hidden, upstream, weights, norm_gains, steering, steer_layer):
    sections = lax.axis_size("section")
    section_index = lax.axis_index("section")
    scaling = norm_gains[0].astype(jnp.float32)
    steer_vec = steering.astype(jnp.float32)
    unsteered_all = hidden[0].astype(jnp.float32)
    moved_all = unsteered_all + steer_vec
    row_count = unsteered_all.shape[1]
    feature_count = unsteered_all.shape[2]
    local_weight = weights[0]
    contract = (((1,), (1,)), ((), ()))

    def regroup(full):
        split = full.reshape(row_count, cols, groups, piece)
        return jnp.swapaxes(split, 1, 2).reshape(row_count, cols * groups * piece)

    groups = lax.axis_size("groups")
    cols = lax.axis_size("col")
    piece = local_weight.shape[1] // groups
    own_piece = lax.dynamic_slice_in_dim(local_weight, lax.axis_index("groups") * piece, piece, 1)
    full_weight = lax.all_gather(own_piece, ("groups", "col"), axis=1, tiled=True)
    ticks = MICRO + sections - 1
    received = jnp.zeros((row_count, feature_count), jnp.bfloat16)
    results = jnp.zeros((MICRO, row_count, feature_count), jnp.bfloat16)
    steer_part = jnp.zeros((feature_count,), jnp.float32)
    slots = jnp.arange(MICRO, dtype=jnp.int32)
    for tick_index in range(ticks):
        micro_index = tick_index - (sections - 1 - section_index)
        active = (micro_index >= 0) & (micro_index < MICRO)
        clipped = jnp.clip(micro_index, 0, MICRO - 1)
        if tick_index < MICRO:
            upstream_block = upstream[tick_index]
        else:
            upstream_block = jnp.zeros_like(upstream[0])
        grad_in = jnp.where(section_index == sections - 1, upstream_block, received)
        unsteered = lax.dynamic_index_in_dim(unsteered_all, clipped, 0, keepdims=False)
        moved = lax.dynamic_index_in_dim(moved_all, clipped, 0, keepdims=False)
        layer_rows = lax.dynamic_index_in_dim(steer_layer, clipped, 0, keepdims=False)
        steered = layer_rows == section_index
        steered_col = steered[:, None]
        normal_grad = lax.dot_general(
            regroup(lax.all_gather(grad_in, "row", axis=1, tiled=True)),
            full_weight,
            contract,
            preferred_element_type=jnp.float32,
        )
        grad_float = grad_in.astype(jnp.float32)
        scaled = scaling * normal_grad
        plain_local = jnp.sum(unsteered * unsteered, -1)
        moved_local = jnp.sum(moved * moved, -1)
        scaled_plain = jnp.sum(scaled * unsteered, -1)
        scaled_moved = jnp.sum(scaled * moved, -1)
        plain_sq, moved_sq, curve_plain, curve_moved = lax.psum(
            (plain_local, moved_local, scaled_plain, scaled_moved), "row"
        )
        norm_plain = jnp.sqrt(plain_sq + epsilon)
        norm_moved = jnp.sqrt(moved_sq + epsilon)
        rescale = norm_plain / norm_moved
        square_sum = jnp.where(
            steered, norm_plain * norm_plain * moved_sq / (norm_moved * norm_moved), plain_sq
        )
        root_mean = jnp.sqrt(square_sum / D + epsilon)
        curvature = jnp.where(steered, rescale * curve_moved, curve_plain)
        rescaled = jnp.where(steered_col, moved * rescale[:, None], unsteered)
        factor = curvature / (D * root_mean**3)
        input_grad = grad_float + scaled / root_mean[:, None] - rescaled * factor[:, None]
        direction = moved / norm_moved[:, None]
        radial = lax.psum(jnp.sum(direction * input_grad, -1), "row")
        tangent = rescale[:, None] * (input_grad - direction * radial[:, None])
        below = jnp.where(
            steered_col, tangent + unsteered / norm_plain[:, None] * radial[:, None], input_grad
        )
        passed = jnp.where(active, below, 0.0).astype(jnp.bfloat16)
        results = jnp.where((slots == micro_index)[:, None, None], passed[None], results)
        steer_part = steer_part + jnp.sum(jnp.where(active & steered_col, tangent, 0.0), 0)
        if tick_index + 1 < ticks:
            received = passed_along(passed, "section", -1)
    steer_total = lax.psum(steer_part, ("section", "col"))
    return (results[None], steer_total / (MICRO * ROWS))


def solution(mesh):
    placed = (
        P("section", None, ("groups", "col"), "row"),
        P(None, ("groups", "col"), "row"),
        P("section", "row", "col"),
        P("section", "row"),
        P(("groups", "row")),
        P(None, ("groups", "col")),
    )
    return jax.shard_map(
        local,
        mesh=mesh,
        in_specs=placed,
        out_specs=(P("section", None, ("groups", "col"), "row"), P(("groups", "row"))),
        check_vma=False,
    )
```

profile of v0, /device:TPU:1, one launch (start us, length us, event | category | flops | bytes accessed | tf_op | source)
XLA Modules:
  0.0 1859.2 jit_solution(14400749378231385533)
XLA Ops:
  7.2 0.0 all-gather.11.cloned.1.call-start
  7.2 3.8 slice_select_fusion
  11.0 0.0 all-gather.11.cloned.1.call-update
  11.0 0.0 all-gather.13.cloned.1.call-start
  11.1 7.7 constant_dynamic-slice_fusion
  18.7 0.0 all-gather.13.cloned.1.call-update
  18.7 0.0 all-gather.7.cloned.1.call-start
  18.8 0.6 copy-done.11
  19.5 0.0 copy-done.13
  19.5 0.0 copy-start.14
  19.5 10.7 convert_element_type.29
  30.2 0.0 copy-done.14
  30.2 0.6 compare_reduce_fusion.2
  30.8 9.0 bitcast_add_fusion
  39.8 53.8 %all-gather.11.cloned.1.call-done = bf16[1,384,8192]{2,1,0:T(8,128)(2,1)} async-done(((bf16[1,384,4096]{2,1,0:T(8,128)(2,1)}), bf16[1,384,8192]{2,1,0:T(8,128)(2,1)}) %all-gather.11.cloned.1.call-update) | async-done | bytes 6291472 | tf_op jit(solution)/shard_map/all_gather | solution.py:59
  93.6 11.2 reshape.112
  104.8 16.4 copy.8
  121.3 1240.8 %all-gather.13.cloned.1.call-done = bf16[1,4096,8192]{2,1,0:T(8,128)(2,1)} async-done(((bf16[1,4096,1024]{2,1,0:T(8,128)(2,1)}), bf16[1,4096,8192]{2,1,0:T(8,128)(2,1)}) %all-gather.13.cloned.1.call-update) | async-done | bytes 67108880 | tf_op jit(solution)/shard_map/all_gather | solution.py:38
  1362.1 36.7 %fusion.10 = (f32[384]{0:T(512)S(1)}, f32[384]{0:T(512)S(1)}, f32[384]{0:T(512)S(1)}, f32[384]{0:T(512)S(1)}, f32[384,4096]{1,0:T(8,128)}) fusion(f32[2,384,4096]{2,1,0:T(8,128)} %bitcast_add_fusion, s32[]{:T(128)S(6)} %min.12, f32[1,2,384,4096]{3,2,1,0:T(8,128)} %convert_element_type.29, bf16[384,8192]{0,1:T(8,128)(2,1)} %bitcast.166, ...), kind=kOutput, calls=%fused_computation.16 | convolution fusion | flops 25783959552 | bytes 92297216 | tf_op jit(solution)/shard_map/dot_general | solution.py:58
  1398.8 3.8 all-reduce.2
  1402.6 0.0 copy-start.5
  1402.7 0.0 copy-start.7
  1402.7 11.2 multiply_reduce_fusion.2
  1413.8 3.8 psum.120
  1417.6 0.0 copy-done.5
  1417.6 0.0 copy-done.7
  1417.6 8.1 fusion.41
  1425.7 0.0 copy-done.9
  1425.8 0.0 copy-start.2
  1425.8 1.7 copy-done.2
  1427.4 5.2 collective-permute-start
  1432.7 4.9 collective-permute-done
  1437.6 3.9 bitcast_select_fusion
  1441.5 0.0 all-gather.7.cloned.1.call-update
  1441.5 0.0 all-gather.9.cloned.1.call-start
  1441.6 81.4 %all-gather.7.cloned.1.call-done = bf16[384,8192]{1,0:T(8,128)(2,1)} async-done(((bf16[384,4096]{1,0:T(8,128)(2,1)}), bf16[384,8192]{1,0:T(8,128)(2,1)}) %all-gather.7.cloned.1.call-update) | async-done | bytes 6291472 | tf_op jit(solution)/shard_map/all_gather | solution.py:59
  1523.0 11.1 reshape.114
  1534.1 16.3 copy.9
  1550.4 36.9 %fusion.21 = (f32[384]{0:T(512)S(1)}, f32[384]{0:T(512)S(1)}, f32[384]{0:T(512)S(1)}, f32[384]{0:T(512)S(1)}, f32[384,4096]{1,0:T(8,128)}) fusion(f32[2,384,4096]{2,1,0:T(8,128)} %bitcast_add_fusion, s32[]{:T(128)S(6)} %min.11, f32[1,2,384,4096]{3,2,1,0:T(8,128)} %convert_element_type.29, bf16[384,8192]{0,1:T(8,128)(2,1)} %bitcast.168, ...), kind=kOutput, calls=%fused_computation.34 | convolution fusion | flops 25783959552 | bytes 92297216 | tf_op jit(solution)/shard_map/dot_general | solution.py:58
  1587.4 3.8 all-reduce.1
  1591.2 0.0 copy-done.1
  1591.2 10.4 multiply_reduce_fusion.1
  1601.7 3.8 psum.123
  1605.4 8.1 fusion.40
  1613.5 0.0 copy-start.4
  1613.6 1.6 copy-done.4
  1615.1 5.4 collective-permute-start.1
  1620.6 4.8 collective-permute-done.1
  1625.4 1.8 broadcast_select_fusion
  1627.3 0.0 all-gather.9.cloned.1.call-update
  1627.3 0.0 copy-done.12
  1627.4 80.2 %all-gather.9.cloned.1.call-done = bf16[384,8192]{1,0:T(8,128)(2,1)} async-done(((bf16[384,4096]{1,0:T(8,128)(2,1)}), bf16[384,8192]{1,0:T(8,128)(2,1)}) %all-gather.9.cloned.1.call-update) | async-done | bytes 6291472 | tf_op jit(solution)/shard_map/all_gather | solution.py:59
  1707.5 11.1 reshape.116
  1718.6 16.2 copy.10
  1734.9 36.7 %fusion.32 = (f32[384]{0:T(512)S(1)}, f32[384]{0:T(512)S(1)}, f32[384]{0:T(512)S(1)}, f32[384]{0:T(512)S(1)}, f32[384,4096]{1,0:T(8,128)}) fusion(f32[2,384,4096]{2,1,0:T(8,128)} %bitcast_add_fusion, s32[]{:T(128)S(6)} %min.10, f32[1,2,384,4096]{3,2,1,0:T(8,128)} %convert_element_type.29, bf16[384,8192]{0,1:T(8,128)(2,1)} %bitcast.167, ...), kind=kOutput, calls=%fused_computation.52 | convolution fusion | flops 25783959552 | bytes 92297216 | tf_op jit(solution)/shard_map/dot_general | solution.py:58
  1771.6 3.8 all-reduce
  1775.5 10.5 multiply_reduce_fusion
  1785.9 3.8 psum.126
  1789.7 9.4 fusion.39
  1799.1 0.0 copy-done
  1799.1 14.4 select_reduce_fusion.1
  1813.6 31.8 %psum.127 = f32[4096]{0:T(1024)S(1)} all-reduce(f32[4096]{0:T(1024)S(1)} %add_add_fusion), channel_id=1, replica_groups=mesh['groups'=2,'section'=2,'row'=2,'col'=4] {'section','col'}, use_global_device_ids=true, to_apply=%region_33.34 | all-reduce | flops 4096 | bytes 32768 | tf_op jit(solution)/shard_map/psum | solution.py:95
  1845.3 0.6 broadcast_multiply_fusion
  1846.0 6.7 select_select_fusion
  (25 shorter events, 0.2 us)
Async XLA Ops:
  7.2 86.4 %all-gather.11.cloned.1.call-start = ((), (), s32[]{:S(2)}) async-start(), calls=%async_computation.2 | async-start | bytes 9437184 | tf_op jit(solution)/shard_map/all_gather | solution.py:59
  11.0 1351.1 %all-gather.13.cloned.1.call-start = ((), (), s32[]{:S(2)}) async-start(), calls=%async_computation.3 | async-start | bytes 75497472 | tf_op jit(solution)/shard_map/all_gather | solution.py:38
  18.7 0.7 copy-start.11
  18.7 0.7 copy-start.13
  18.7 1504.2 %all-gather.7.cloned.1.call-start = ((), (), s32[]{:S(2)}) async-start(), calls=%async_computation | async-start | bytes 9437184 | tf_op jit(solution)/shard_map/all_gather | solution.py:59
  19.5 10.7 copy-start.14
  1402.6 15.0 copy-start.5
  1402.7 15.0 copy-start.7
  1417.6 8.1 copy-start.9
  1425.8 1.7 copy-start.2
  1427.4 10.1 collective-permute-start
  1441.5 266.0 %all-gather.9.cloned.1.call-start = ((), (), s32[]{:S(2)}) async-start(), calls=%async_computation.1 | async-start | bytes 9437184 | tf_op jit(solution)/shard_map/all_gather | solution.py:59
  1550.4 40.8 %copy-start.1 = (bf16[384,4096]{1,0:T(8,128)(2,1)S(1)}, bf16[384,4096]{1,0:T(8,128)(2,1)}, u32[]{:S(2)}) copy-start(bf16[384,4096]{1,0:T(8,128)(2,1)} %bitcast_select_fusion) | copy-start | bytes 9437188
  1613.5 1.6 copy-start.4
  1615.1 12.2 copy-start.12
  1615.1 10.3 collective-permute-start.1
  1789.7 9.4 copy-start
  1789.7 9.4 copy-start.6
  1789.7 9.4 copy-start.8
  1789.7 9.4 copy-start.10
  1799.1 46.9 %copy-start.3 = (bf16[384,4096]{1,0:T(8,128)(2,1)S(1)}, bf16[384,4096]{1,0:T(8,128)(2,1)}, u32[]{:S(2)}) copy-start(bf16[384,4096]{1,0:T(8,128)(2,1)} %copy-done.2) | copy-start | bytes 9437188
Sparse Core Ops, SparseCore 0:
  11.1 82.4 all-gather.10
  95.1 1266.8 all-gather.12
  1441.6 81.2 all-gather.6
  1627.4 80.0 all-gather.8
where the time goes:
time: 1860 us
  waiting for transfers between devices  1470 us (79%)
  matrix products  110 us (6%)
  other arithmetic  109 us (6%)
  local copies, waits for them, and re-layouts  94.1 us (5%)
  blocking collectives  54.5 us (3%)
    all_gather x1, waiting for transfers between devices, local(): lax.all_gather(own_piece, ('groups', 'col'), axis=1, tiled=True)  1240 us
    all_gather x3, waiting for transfers between devices, local(): lax.all_gather(grad_in, 'row', axis=1, tiled=True)  215 us
    dot_general x3, matrix products, local(): lax.dot_general(regroup(lax.all_gather(grad_in, 'row', axis=1, tiled=True...  110 us
    reshape x6, local copies, waits for them, and re-layouts, regroup(): split = full.reshape(row_count, cols, groups, piece)  82.5 us
  transfers between devices with their start and end apart: 6, of which 6 were waited for; matrix products, arithmetic and copies ran while one was open for 3% of the time, Pallas kernels for 0%

commit v1 on v0

--- a/solution.py
+++ b/solution.py
@@ -7,6 +7,18 @@
 ROWS = 1536
 MICRO = 2
 epsilon = 1e-06
+
+
+def gather_by_bits(x, axis, dim):
+    ways, here, step = (lax.axis_size(axis), lax.axis_index(axis), x.shape[dim])
+    line, have = (x, 1)
+    while have < ways:
+        line = jnp.concatenate(
+            [line, lax.ppermute(line, axis, [(d, (d - have) % ways) for d in range(ways)])],
+            axis=dim,
+        )
+        have = 2 * have
+    return jnp.roll(line, here * step, axis=dim)
 
 
 def passed_along(value, axis, steps):
@@ -56,7 +68,7 @@
         steered = layer_rows == section_index
         steered_col = steered[:, None]
         normal_grad = lax.dot_general(
-            regroup(lax.all_gather(grad_in, "row", axis=1, tiled=True)),
+            regroup(gather_by_bits(grad_in, "row", 1)),
             full_weight,
             contract,
             preferred_element_type=jnp.float32,

time: 1860 us -> 1760 us (0.946)
  waiting for transfers between devices: 1470 us -> 1370 us
  local copies, waits for them, and re-layouts: 94.1 us -> 49.9 us
    all_gather x3 -> x0, waiting for transfers between devices: 215 us -> none  [local(): lax.all_gather(grad_in, 'row', axis=1, tiled=True)]
    ppermute x0 -> x3, waiting for transfers between devices: none -> 184 us  [gather_by_bits(): lax.ppermute(line, axis, [(d, (d - have) % ways) for d in range(ways)])]
    reshape x6 -> x0, local copies, waits for them, and re-layouts: 82.5 us -> none  [regroup(): split = full.reshape(row_count, cols, groups, piece)]
    all_gather x1, waiting for transfers between devices: 1240 us -> 1170 us  [local(): lax.all_gather(own_piece, ('groups', 'col'), axis=1, tiled=True)]
    dynamic_slice x0 -> x3, local copies, waits for them, and re-layouts: none -> 26 us  [gather_by_bits(): return jnp.roll(line, here * step, axis=dim)]
    concatenate x0 -> x3, other arithmetic: none -> 22.2 us  [gather_by_bits(): return jnp.roll(line, here * step, axis=dim)]
where the time goes in v1:
time: 1760 us; the launch traced here: 1750 us
  waiting for transfers between devices  1370 us (78%)
  other arithmetic  127 us (7%)
  matrix products  116 us (7%)
  blocking collectives  57 us (3%)
  local copies, waits for them, and re-layouts  49.9 us (3%)
    all_gather x1, waiting for transfers between devices, local(): lax.all_gather(own_piece, ('groups', 'col'), axis=1, tiled=True)  1170 us
    ppermute x3, waiting for transfers between devices, gather_by_bits(): lax.ppermute(line, axis, [(d, (d - have) % ways) for d in range(ways)])  184 us
    dot_general x3, matrix products, local(): lax.dot_general(regroup(gather_by_bits(grad_in, 'row', 1)), full_weight,...  116 us
  transfers between devices with their start and end apart: 6, of which 6 were waited for; matrix products, arithmetic and copies ran while one was open for 3% of the time, Pallas kernels for 0%

profile of v1, /device:TPU:1, one launch (start us, length us, event | category | flops | bytes accessed | tf_op | source)
XLA Modules:
  0.0 1748.6 jit_solution(14925449148972596899)
XLA Ops:
  7.2 0.0 all-gather.3.cloned.1.call-start
  7.2 7.7 constant_dynamic-slice_fusion
  14.9 0.0 all-gather.3.cloned.1.call-update
  14.9 2.1 select_bitcast_fusion
  17.0 2.1 collective-permute-start
  19.1 0.0 copy-done.12
  19.1 0.0 copy-done.15
  19.2 0.0 copy-start.16
  19.2 10.1 convert_element_type.29
  29.2 0.0 copy-done.16
  29.2 0.6 compare_reduce_fusion.2
  29.8 9.6 bitcast_add_fusion
  39.4 47.6 %collective-permute-done = bf16[384,4096]{1,0:T(8,128)(2,1)} collective-permute-done((bf16[384,4096]{1,0:T(8,128)(2,1)S(1)}, bf16[384,4096]{1,0:T(8,128)(2,1)}, u32[]{:S(2)}, u32[]{:S(2)}) %collective-permute-start) | collective-permute-done | bytes 3145760 | tf_op jit(solution)/shard_map/ppermute | solution.py:17
  87.0 7.4 fusion.13
  94.4 8.7 copy.8
  103.1 6.2 copy.9
  109.3 1174.7 %all-gather.3.cloned.1.call-done = bf16[1,4096,8192]{2,1,0:T(8,128)(2,1)} async-done(((bf16[1,4096,1024]{2,1,0:T(8,128)(2,1)}), bf16[1,4096,8192]{2,1,0:T(8,128)(2,1)}) %all-gather.3.cloned.1.call-update) | async-done | bytes 67108880 | tf_op jit(solution)/shard_map/all_gather | solution.py:50
  1284.0 36.7 %fusion.19 = (f32[384]{0:T(512)S(1)}, f32[384]{0:T(512)S(1)}, f32[384]{0:T(512)S(1)}, f32[384]{0:T(512)S(1)}, f32[384,4096]{1,0:T(8,128)}) fusion(f32[2,384,4096]{2,1,0:T(8,128)} %bitcast_add_fusion, s32[]{:T(128)S(6)} %min.12, f32[1,2,384,4096]{3,2,1,0:T(8,128)} %convert_element_type.29, bf16[384,8192]{0,1:T(8,128)(2,1)} %bitcast.172, ...), kind=kOutput, calls=%fused_computation.36 | convolution fusion | flops 25783959552 | bytes 92297216 | tf_op jit(solution)/shard_map/dot_general | solution.py:70
  1320.8 3.8 all-reduce.2
  1324.6 0.0 copy-start.6
  1324.6 0.0 copy-start.8
  1324.6 11.2 multiply_reduce_fusion.2
  1335.8 4.2 psum.120
  1340.0 0.0 copy-done.6
  1340.0 0.0 copy-done.8
  1340.0 8.1 fusion.50
  1348.2 0.0 copy-done.10
  1348.2 0.0 copy-start.1
  1348.2 5.1 collective-permute-start.1
  1353.3 5.1 collective-permute-done.1
  1358.4 0.0 copy-done.1
  1358.4 2.3 bitcast_select_fusion
  1360.7 1.3 collective-permute-start.2
  1361.9 68.2 %collective-permute-done.2 = bf16[384,4096]{1,0:T(8,128)(2,1)} collective-permute-done((bf16[384,4096]{1,0:T(8,128)(2,1)S(1)}, bf16[384,4096]{1,0:T(8,128)(2,1)}, u32[]{:S(2)}, u32[]{:S(2)}) %collective-permute-start.2) | collective-permute-done | bytes 3145760 | tf_op jit(solution)/shard_map/ppermute | solution.py:17
  1430.1 7.5 fusion.10
  1437.6 8.6 copy.10
  1446.2 3.4 copy.11
  1449.6 0.0 copy-start.13
  1449.7 39.6 %fusion.30 = (f32[384]{0:T(512)S(1)}, f32[384]{0:T(512)S(1)}, f32[384]{0:T(512)S(1)}, f32[384]{0:T(512)S(1)}, f32[384,4096]{1,0:T(8,128)}) fusion(f32[2,384,4096]{2,1,0:T(8,128)} %bitcast_add_fusion, s32[]{:T(128)S(6)} %min.11, f32[1,2,384,4096]{3,2,1,0:T(8,128)} %convert_element_type.29, bf16[384,8192]{0,1:T(8,128)(2,1)S(1)} %bitcast.174, ...), kind=kOutput, calls=%fused_computation.54 | convolution fusion | flops 25783959552 | bytes 92297216 | tf_op jit(solution)/shard_map/dot_general | solution.py:70
  1489.3 3.8 all-reduce.1
  1493.1 0.0 copy-done.13
  1493.1 10.4 multiply_reduce_fusion.1
  1503.6 3.9 psum.123
  1507.5 8.1 fusion.49
  1515.6 1.6 copy-done.3
  1517.2 5.7 collective-permute-start.3
  1522.9 5.1 collective-permute-done.3
  1528.0 1.6 copy-done.4
  1529.6 0.2 broadcast_select_fusion
  1529.9 1.3 collective-permute-start.4
  1531.2 68.1 %collective-permute-done.4 = bf16[384,4096]{1,0:T(8,128)(2,1)} collective-permute-done((bf16[384,4096]{1,0:T(8,128)(2,1)S(1)}, bf16[384,4096]{1,0:T(8,128)(2,1)}, u32[]{:S(2)}, u32[]{:S(2)}) %collective-permute-start.4) | collective-permute-done | bytes 3145760 | tf_op jit(solution)/shard_map/ppermute | solution.py:17
  1599.3 7.4 fusion.7
  1606.7 8.7 copy.12
  1615.4 3.4 copy.13
  1618.8 39.8 %fusion.41 = (f32[384]{0:T(512)S(1)}, f32[384]{0:T(512)S(1)}, f32[384]{0:T(512)S(1)}, f32[384]{0:T(512)S(1)}, f32[384,4096]{1,0:T(8,128)}) fusion(f32[2,384,4096]{2,1,0:T(8,128)} %bitcast_add_fusion, s32[]{:T(128)S(6)} %min.10, f32[1,2,384,4096]{3,2,1,0:T(8,128)} %convert_element_type.29, bf16[384,8192]{0,1:T(8,128)(2,1)S(1)} %bitcast.173, ...), kind=kOutput, calls=%fused_computation.72 | convolution fusion | flops 25783959552 | bytes 92297216 | tf_op jit(solution)/shard_map/dot_general | solution.py:70
  1658.6 3.8 all-reduce
  1662.5 10.5 multiply_reduce_fusion
  1672.9 4.0 psum.126
  1676.9 9.4 fusion.48
  1686.3 0.0 copy-done.7
  1686.4 14.4 select_reduce_fusion.1
  1700.8 33.4 %psum.127 = f32[4096]{0:T(1024)S(1)} all-reduce(f32[4096]{0:T(1024)S(1)} %add_add_fusion), channel_id=1, replica_groups=mesh['groups'=2,'section'=2,'row'=2,'col'=4] {'section','col'}, use_global_device_ids=true, to_apply=%region_33.35 | all-reduce | flops 4096 | bytes 32768 | tf_op jit(solution)/shard_map/psum | solution.py:107
  1734.2 0.6 broadcast_multiply_fusion
  1734.8 6.7 select_select_fusion
  (29 shorter events, 0.2 us)
Async XLA Ops:
  7.2 1276.9 %all-gather.3.cloned.1.call-start = ((), (), s32[]{:S(2)}) async-start(), calls=%async_computation | async-start | bytes 75497472 | tf_op jit(solution)/shard_map/all_gather | solution.py:50
  14.9 4.2 copy-start.12
  14.9 4.3 copy-start.15
  17.0 70.0 %collective-permute-start = (bf16[384,4096]{1,0:T(8,128)(2,1)S(1)}, bf16[384,4096]{1,0:T(8,128)(2,1)}, u32[]{:S(2)}, u32[]{:S(2)}) collective-permute-start(bf16[384,4096]{1,0:T(8,128)(2,1)S(1)} %select_bitcast_fusion), channel_id=1, source_target_pairs={{0,4},{4,0},{1,5},{5,1},{2,6},{6,2},{3,7},{7,3},{8,12},{12,8},{9,1... | collective-permute-start | bytes 9437192 | tf_op jit(solution)/shard_map/ppermute | solution.py:17
  19.2 10.1 copy-start.16
  1324.6 15.4 copy-start.6
  1324.6 15.4 copy-start.8
  1340.0 8.1 copy-start.10
  1348.2 10.2 copy-start.1
  1348.2 10.2 collective-permute-start.1
  1360.7 69.5 %collective-permute-start.2 = (bf16[384,4096]{1,0:T(8,128)(2,1)S(1)}, bf16[384,4096]{1,0:T(8,128)(2,1)}, u32[]{:S(2)}, u32[]{:S(2)}) collective-permute-start(bf16[384,4096]{1,0:T(8,128)(2,1)S(1)} %bitcast_select_fusion), channel_id=1, source_target_pairs={{0,4},{4,0},{1,5},{5,1},{2,6},{6,2},{3,7},{7,3},{8,12},{12,8},{9,1... | collective-permute-start | bytes 9437192 | tf_op jit(solution)/shard_map/ppermute | solution.py:17
  1449.6 43.5 %copy-start.13 = (pred[384]{0:T(512)(128)(4,1)S(1)}, pred[384]{0:T(512)(128)(4,1)}, u32[]{:S(2)}) copy-start(pred[384]{0:T(512)(128)(4,1)} %get-tuple-element.26) | copy-start | bytes 1156
  1515.6 1.6 copy-start.3
  1517.2 13.9 copy-start.14
  1517.2 10.8 collective-permute-start.3
  1528.0 1.6 copy-start.4
  1529.9 69.5 %collective-permute-start.4 = (bf16[384,4096]{1,0:T(8,128)(2,1)S(1)}, bf16[384,4096]{1,0:T(8,128)(2,1)}, u32[]{:S(2)}, u32[]{:S(2)}) collective-permute-start(bf16[384,4096]{1,0:T(8,128)(2,1)S(1)} %broadcast_select_fusion), channel_id=1, source_target_pairs={{0,4},{4,0},{1,5},{5,1},{2,6},{6,2},{3,7},{7,3},{8,12},{12,8},{9,1... | collective-permute-start | bytes 9437192 | tf_op jit(solution)/shard_map/ppermute | solution.py:17
  1618.8 43.6 %copy-start.5 = (bf16[384,4096]{1,0:T(8,128)(2,1)S(1)}, bf16[384,4096]{1,0:T(8,128)(2,1)}, u32[]{:S(2)}) copy-start(bf16[384,4096]{1,0:T(8,128)(2,1)} %copy-done.4) | copy-start | bytes 9437188
  1676.9 9.4 copy-start
  1676.9 9.4 copy-start.7
  1676.9 9.4 copy-start.9
  1676.9 9.4 copy-start.11
  1686.3 48.4 %copy-start.2 = (bf16[384,4096]{1,0:T(8,128)(2,1)S(1)}, bf16[384,4096]{1,0:T(8,128)(2,1)}, u32[]{:S(2)}) copy-start(bf16[384,4096]{1,0:T(8,128)(2,1)} %copy-done.1) | copy-start | bytes 9437188
Sparse Core Ops, SparseCore 0:
  15.0 1268.9 all-gather.2
